TPU v7x, 32 devices: a whole 2x2x4 slice. The times are simulated.
32 devices in a mesh: groups: 2 (over x), col: 16 (over z, y, core).
Axes of the slice: x: 2, y: 2, z: 4, core: 2. Of those that a mesh axis runs over, the one named last changes fastest.
Arguments:
- slab: float32 [2, 2048, 4096], P(None, 'groups', 'col'), parts along dimension 1, may hold values from -6 to 6
- block_on: int32 [16, 32], P('groups', 'col'), parts along dimension 0, may hold values 0 or 1
- block_band: int32 [16, 32], P('groups', 'col'), parts along dimension 0, may hold values from 0 to 3
- band_gain: float32 [4], replicated, may hold values from 0.25 to 2
Outputs:
- spectra: float32 [2, 2048, 4096], P(None, 'groups', 'col'), parts along dimension 1
There are 2 independent parts, one for each index of `groups`. A program takes and returns all parts, laid end to end along the dimension named above; an argument that names none is the same for every part. Nothing has to cross between parts.
All inputs are finite; a program needn't handle non-finite values. No bound on the sum of `block_on` on one device may be relied on, other than what follows from the above.
Results may differ from a plain program's by a relative error of at most 0.00007.
Values sent between devices are 32-bit elements; how exact they have to be, the bound alone decides.
No kernel may reach another device: no remote copies, remote signals or barrier semaphores. Data moves between devices by JAX's collectives and lax.ppermute only.
A program may use at most 64 MiB of HBM per device.

v0:
```python
import math
import jax
import jax.numpy as jnp
from jax import lax
from jax.sharding import PartitionSpec as P

BLOCK = 128


def phase_table(first_index, second_index, length):
    product = first_index[:, None] * second_index[None, :] % length
    angles = product.astype(jnp.float32) * (2.0 * math.pi / length)
    return (jnp.cos(angles), -jnp.sin(angles))


def contract(stacked, table, formula):
    cosine_table, sine_table = table
    real_part = jnp.einsum(
        formula, stacked[0], cosine_table, precision=lax.Precision.HIGHEST
    ) - jnp.einsum(formula, stacked[1], sine_table, precision=lax.Precision.HIGHEST)
    imag_part = jnp.einsum(
        formula, stacked[0], sine_table, precision=lax.Precision.HIGHEST
    ) + jnp.einsum(formula, stacked[1], cosine_table, precision=lax.Precision.HIGHEST)
    return jnp.stack([real_part, imag_part])


def rotate(stacked, table):
    cosine_table, sine_table = table
    real_part = stacked[0] * cosine_table - stacked[1] * sine_table
    imag_part = stacked[0] * sine_table + stacked[1] * cosine_table
    return jnp.stack([real_part, imag_part])


def shards(slab, block_on, block_band, band_gain):
    devices = lax.axis_size("col")
    rows_total = slab.shape[1]
    shard_cols = slab.shape[2]
    length = shard_cols * devices
    rows_here = rows_total // devices
    factor = 1.0 / math.sqrt(length)
    first_len = BLOCK
    second_len = length // first_len
    first_iota = jnp.arange(first_len, dtype=jnp.int32)
    second_iota = jnp.arange(second_len, dtype=jnp.int32)
    table_one = phase_table(first_iota, first_iota, first_len)
    table_middle = phase_table(first_iota, second_iota, length)
    table_two = phase_table(second_iota, second_iota, second_len)
    received = lax.all_to_all(
        slab.reshape(2, devices, rows_here, shard_cols),
        "col",
        split_axis=1,
        concat_axis=3,
        tiled=True,
    )
    row_count = received.shape[2]
    square = received[:, 0].reshape(2, row_count, first_len, second_len)
    mixture = contract(square, table_one, "rab,ak->rkb")
    mixture = rotate(mixture, table_middle)
    result = contract(mixture, table_two, "rkb,bm->rmk")
    whole = result.reshape(2, 1, row_count, length)
    whole = whole.reshape(2, rows_here, devices, shard_cols)
    spectrum = lax.all_to_all(whole, "col", split_axis=2, concat_axis=1, tiled=True).reshape(
        2, rows_total, shard_cols
    )
    choose = (block_band[..., None] == jnp.arange(band_gain.shape[0], dtype=jnp.int32)).astype(
        jnp.float32
    )
    weight = block_on.astype(jnp.float32) * jnp.sum(choose * band_gain, axis=-1) * factor
    row_blocks = rows_total // BLOCK
    col_blocks = shard_cols // BLOCK
    masked = (
        spectrum.reshape(2, row_blocks, BLOCK, col_blocks, BLOCK) * weight[None, :, None, :, None]
    )
    return masked.reshape(2, rows_total, shard_cols)


def solution(mesh):
    placed = (P(None, "groups", "col"), P("groups", "col"), P("groups", "col"), P())
    return jax.shard_map(
        shards, mesh=mesh, in_specs=placed, out_specs=P(None, "groups", "col"), check_vma=False
    )
```

profile of v0, /device:TPU:13, one launch (start us, length us, event | category | flops | bytes accessed | tf_op | source)
XLA Modules:
  0.0 138.4 jit_solution(2403043482625478237)
XLA Ops:
  0.0 3.1 %copy.54 = f32[2,16,64,256]{3,2,0,1:T(8,128)} copy(f32[2,16,64,256]{3,2,1,0:T(8,128)} %bitcast.56) | data formatting | bytes 4194304 | tf_op jit(solution)/shard_map/reshape | solution.py:49
  3.1 6.5 %all-to-all-start = ((f32[2,16,64,256]{3,2,0,1:T(8,128)}), f32[2,16,64,256]{3,2,0,1:T(8,128)S(1)}, u32[]{:S(2)}, u32[]{:S(2)}) async-start(f32[2,16,64,256]{3,2,0,1:T(8,128)} %copy.54), calls=%async_computation | async-start | bytes 4194304 | tf_op jit(solution)/shard_map/all_to_all | solution.py:48
  9.7 0.1 sine_negate_fusion.4
  9.7 47.3 %all-to-all-done = f32[2,16,64,256]{3,2,0,1:T(8,128)S(1)} async-done(((f32[2,16,64,256]{3,2,0,1:T(8,128)}), f32[2,16,64,256]{3,2,0,1:T(8,128)S(1)}, u32[]{:S(2)}, u32[]{:S(2)}) %all-to-all-start) | async-done | bytes 2097184 | tf_op jit(solution)/shard_map/all_to_all | solution.py:48
  57.1 1.2 fusion.79
  58.2 0.6 copy.55
  58.8 1.3 copy.56
  60.1 0.0 copy-start.1
  60.1 1.2 fusion.11
  61.4 2.2 %fusion.15 = f32[128,64,32]{0,1,2:T(8,128)} fusion(f32[64,128,32]{1,0,2:T(8,128)S(1)} %copy.56), kind=kOutput, calls=%fused_computation.27 | convolution fusion | flops 402882560 | bytes 2097152 | tf_op jit(solution)/shard_map/rab,ak->rkb/dot_general | solution.py:18
  63.6 0.0 copy-done.1
  63.6 1.9 %copy.57 = f32[1,1,64,16,256]{2,4,3,1,0:T(8,128)} copy(f32[1,1,64,16,256]{4,2,0,3,1:T(8,128)S(1)} %copy-done.1) | data formatting | bytes 2097152 | tf_op jit(solution)/shard_map/slice | solution.py:20
  65.5 2.7 %copy.58 = f32[64,128,32]{1,0,2:T(8,128)S(1)} copy(f32[64,128,32]{0,2,1:T(8,128)} %bitcast.52) | data formatting | bytes 2097152 | tf_op jit(solution)/shard_map/squeeze | solution.py:20
  68.2 0.0 copy-start
  68.2 1.3 convolution_add_fusion.1
  69.5 0.0 copy-done
  69.5 1.4 %add_bitcast_fusion = (f32[64,128,32]{1,0,2:T(8,128)S(1)}, f32[64,128,32]{1,0,2:T(8,128)S(1)}) fusion(f32[128,64,32]{0,1,2:T(8,128)S(1)} %convolution_add_fusion.1, f32[128,32]{0,1:T(8,128)S(1)} %get-tuple-element.9, f32[128,32]{0,1:T(8,128)S(1)} %get-tuple-element.10, f32[128,64,32]{0,1,2:T(8,128)S(1)} %copy-done, f32[64,128,32]{1,0,2:T(8,128)S(1)} %copy.58), kind=kOutput, calls=%fused_computation.9 | convolution fusion | flops 404733952 | bytes 5275648 | tf_op jit(solution)/shard_map/rab,ak->rkb/dot_general | solution.py:20
  70.9 1.6 %fusion.6 = f32[32,64,128]{2,0,1:T(8,128)S(1)} fusion(f32[64,128,32]{1,0,2:T(8,128)S(1)} %get-tuple-element.6), kind=kOutput, calls=%fused_computation.15 | convolution fusion | flops 100677632 | bytes 2097152 | tf_op jit(solution)/shard_map/rkb,bm->rmk/dot_general | solution.py:18
  72.5 1.6 %fusion.4 = f32[32,64,128]{2,0,1:T(8,128)S(1)} fusion(f32[64,128,32]{1,0,2:T(8,128)S(1)} %get-tuple-element.6), kind=kOutput, calls=%fused_computation.13 | convolution fusion | flops 100678656 | bytes 2097152 | tf_op jit(solution)/shard_map/rkb,bm->rmk/dot_general | solution.py:21
  74.1 1.8 %fusion.1 = f32[64,32,128]{2,1,0:T(8,128)S(1)} fusion(f32[32,64,128]{2,0,1:T(8,128)S(1)} %fusion.6, f32[64,128,32]{1,0,2:T(8,128)S(1)} %get-tuple-element.5), kind=kOutput, calls=%fused_computation.5 | convolution fusion | flops 100940800 | bytes 3145728 | tf_op jit(solution)/shard_map/rkb,bm->rmk/dot_general | solution.py:20
  75.9 1.3 stack.9
  77.1 2.8 %copy.65 = f32[1,64,16,256]{3,1,0,2:T(8,128)} copy(f32[1,64,16,256]{3,2,1,0:T(8,128)} %stack.9) | data formatting | bytes 2097152 | tf_op jit(solution)/shard_map/stack | solution.py:24
  79.9 1.6 %fusion = f32[64,32,128]{2,1,0:T(8,128)S(1)} fusion(f32[32,64,128]{2,0,1:T(8,128)S(1)} %fusion.4, f32[64,128,32]{1,0,2:T(8,128)S(1)} %get-tuple-element.5), kind=kOutput, calls=%fused_computation.3 | convolution fusion | flops 100939776 | bytes 3145728 | tf_op jit(solution)/shard_map/rkb,bm->rmk/dot_general | solution.py:23
  81.5 0.0 copy-start.2
  81.6 0.3 stack.10
  81.9 0.6 copy.66
  82.5 0.3 copy-done.2
  82.8 1.5 %pad_maximum_fusion = f32[2,64,16,256]{3,1,0,2:T(8,128)} fusion(f32[1,64,16,256]{3,1,0,2:T(8,128)S(1)} %copy.66, f32[1,64,16,256]{3,1,0,2:T(8,128)S(1)} %copy-done.2), kind=kLoop, calls=%fused_computation | loop fusion | flops 524288 | bytes 4194304 | tf_op jit(solution)/shard_map/stack | solution.py:24
  84.2 0.0 copy-start.4
  84.2 0.0 copy-start.5
  84.2 0.0 copy-start.3
  84.2 4.9 %all-to-all-start.1 = ((f32[2,64,16,256]{3,1,0,2:T(8,128)}), f32[2,64,16,256]{3,1,0,2:T(8,128)S(1)}, u32[]{:S(2)}, u32[]{:S(2)}) async-start(f32[2,64,16,256]{3,1,0,2:T(8,128)} %pad_maximum_fusion), calls=%async_computation.1 | async-start | bytes 4194304 | tf_op jit(solution)/shard_map/all_to_all | solution.py:62
  89.2 0.0 copy-done.4
  89.2 0.0 copy-done.5
  89.2 0.1 select_reduce_fusion
  89.3 0.0 copy-done.3
  89.3 0.1 copy.68
  89.4 0.3 mul.231
  89.7 0.1 copy.79
  89.8 46.8 %all-to-all-done.1 = f32[2,64,16,256]{3,1,0,2:T(8,128)S(1)} async-done(((f32[2,64,16,256]{3,1,0,2:T(8,128)}), f32[2,64,16,256]{3,1,0,2:T(8,128)S(1)}, u32[]{:S(2)}, u32[]{:S(2)}) %all-to-all-start.1) | async-done | bytes 2097184 | tf_op jit(solution)/shard_map/all_to_all | solution.py:62
  136.6 0.2 copy.67
  136.8 1.5 %bitcast_multiply_fusion = f32[2,1024,256]{2,1,0:T(8,128)} fusion(f32[2,64,16,256]{3,1,2,0:T(8,128)S(1)} %copy.67, f32[1024,256]{1,0:T(8,128)S(1)} %bitcast.54), kind=kLoop, calls=%fused_computation.1 | loop fusion | flops 524288 | bytes 5242880 | tf_op jit(solution)/shard_map/mul | solution.py:72
  (1 shorter events, 0.0 us)
Async XLA Ops:
  3.1 53.9 %all-to-all-start = ((f32[2,16,64,256]{3,2,0,1:T(8,128)}), f32[2,16,64,256]{3,2,0,1:T(8,128)S(1)}, u32[]{:S(2)}, u32[]{:S(2)}) async-start(f32[2,16,64,256]{3,2,0,1:T(8,128)} %copy.54), calls=%async_computation | async-start | bytes 4194304 | tf_op jit(solution)/shard_map/all_to_all | solution.py:48
  60.1 3.5 %copy-start.1 = (f32[1,1,64,16,256]{4,2,0,3,1:T(8,128)S(1)}, f32[1,1,64,16,256]{4,2,0,3,1:T(8,128)}, u32[]{:S(2)}) copy-start(f32[1,1,64,16,256]{4,2,0,3,1:T(8,128)} %get-tuple-element.7) | copy-start | bytes 3145732
  68.2 1.3 copy-start
  81.5 1.2 copy-start.2
  84.2 5.0 %copy-start.4 = (s32[8,2]{0,1:T(2,128)S(1)}, s32[8,2]{0,1:T(2,128)}, u32[]{:S(2)}) copy-start(s32[8,2]{0,1:T(2,128)} %param.6) | copy-start | bytes 196
  84.2 5.0 %copy-start.5 = (f32[4]{0:T(128)S(1)}, f32[4]{0:T(128)}, u32[]{:S(2)}) copy-start(f32[4]{0:T(128)} %param.7) | copy-start | bytes 52
  84.2 5.0 %copy-start.3 = (s32[8,2]{0,1:T(2,128)S(1)}, s32[8,2]{0,1:T(2,128)}, u32[]{:S(2)}) copy-start(s32[8,2]{0,1:T(2,128)} %param.5) | copy-start | bytes 196
  84.2 52.4 %all-to-all-start.1 = ((f32[2,64,16,256]{3,1,0,2:T(8,128)}), f32[2,64,16,256]{3,1,0,2:T(8,128)S(1)}, u32[]{:S(2)}, u32[]{:S(2)}) async-start(f32[2,64,16,256]{3,1,0,2:T(8,128)} %pad_maximum_fusion), calls=%async_computation.1 | async-start | bytes 4194304 | tf_op jit(solution)/shard_map/all_to_all | solution.py:62
where the time goes:
time: 139 us; the launch traced here: 138 us
  waiting for transfers between devices  94.1 us (68%)
  local copies, waits for them, and re-layouts  16.8 us (12%)
  matrix products  12.7 us (9%)
  starting transfers between devices  11.5 us (8%)
  other arithmetic  3.18 us (2%)
    all_to_all x1, waiting for transfers between devices, shards(): lax.all_to_all(slab.reshape(2, devices, rows_here, shard_cols), 'col', sp...  47.3 us
    all_to_all x1, waiting for transfers between devices, shards(): lax.all_to_all(whole, 'col', split_axis=2, concat_axis=1, tiled=True)  46.8 us
    all_to_all x1, starting transfers between devices, shards(): lax.all_to_all(slab.reshape(2, devices, rows_here, shard_cols), 'col', sp...  6.52 us
    another operation x4, local copies, waits for them, and re-layouts, contract(): return jnp.stack([real_part, imag_part])  4.98 us
    all_to_all x1, starting transfers between devices, shards(): lax.all_to_all(whole, 'col', split_axis=2, concat_axis=1, tiled=True)  4.94 us
    dot_general x2, matrix products, contract(): jnp.einsum(formula, stacked[0], cosine_table, precision=lax.Precision.HIG...  3.8 us
    dot_general x2, matrix products, contract(): jnp.einsum(formula, stacked[1], sine_table, precision=lax.Precision.HIGHEST)  3.18 us
    reshape x1, local copies, waits for them, and re-layouts, shards(): slab.reshape(2, devices, rows_here, shard_cols)  3.13 us
  transfers between devices with their start and end apart: 2, of which 2 were waited for; matrix products, arithmetic and copies ran while one was open for 0% of the time, Pallas kernels for 0%

commit v1 on v0

--- a/solution.py
+++ b/solution.py
@@ -45,12 +45,18 @@
     table_one = phase_table(first_iota, first_iota, first_len)
     table_middle = phase_table(first_iota, second_iota, length)
     table_two = phase_table(second_iota, second_iota, second_len)
-    received = lax.all_to_all(
-        slab.reshape(2, devices, rows_here, shard_cols),
-        "col",
-        split_axis=1,
-        concat_axis=3,
-        tiled=True,
+    received = jnp.concatenate(
+        lax.all_to_all(
+            jnp.stack(
+                jnp.split(
+                    slab.reshape(2, devices, rows_here, shard_cols), lax.axis_size("col"), axis=1
+                )
+            ),
+            "col",
+            0,
+            0,
+        ),
+        axis=3,
     )
     row_count = received.shape[2]
     square = received[:, 0].reshape(2, row_count, first_len, second_len)

time: 139 us -> 145 us (1.043)
  local copies, waits for them, and re-layouts: 16.8 us -> 22.6 us
    unnamed x13 -> x32, local copies, waits for them, and re-layouts: 0.39 us -> 9.3 us
    reshape x1 -> x0, local copies, waits for them, and re-layouts: 3.13 us -> none  [shards(): slab.reshape(2, devices, rows_here, shard_cols)]
where the time goes in v1:
time: 145 us; the launch traced here: 144 us
  waiting for transfers between devices  94.1 us (65%)
  local copies, waits for them, and re-layouts  22.6 us (16%)
  matrix products  12.7 us (9%)
  starting transfers between devices  11.4 us (8%)
  other arithmetic  3.18 us (2%)
    all_to_all x1, waiting for transfers between devices, shards(): lax.all_to_all(jnp.stack(jnp.split(slab.reshape(2, devices, rows_here, sh...  47.3 us
    all_to_all x1, waiting for transfers between devices, shards(): lax.all_to_all(whole, 'col', split_axis=2, concat_axis=1, tiled=True)  46.8 us
    unnamed x32, local copies, waits for them, and re-layouts  9.3 us
    all_to_all x1, starting transfers between devices, shards(): lax.all_to_all(jnp.stack(jnp.split(slab.reshape(2, devices, rows_here, sh...  6.52 us
    another operation x4, local copies, waits for them, and re-layouts, contract(): return jnp.stack([real_part, imag_part])  4.98 us
    all_to_all x1, starting transfers between devices, shards(): lax.all_to_all(whole, 'col', split_axis=2, concat_axis=1, tiled=True)  4.91 us
    dot_general x2, matrix products, contract(): jnp.einsum(formula, stacked[0], cosine_table, precision=lax.Precision.HIG...  3.8 us
    dot_general x2, matrix products, contract(): jnp.einsum(formula, stacked[1], sine_table, precision=lax.Precision.HIGHEST)  3.18 us
  transfers between devices with their start and end apart: 2, of which 2 were waited for; matrix products, arithmetic and copies ran while one was open for 0% of the time, Pallas kernels for 0%

profile of v1, /device:TPU:13, one launch (start us, length us, event | category | flops | bytes accessed | tf_op | source)
XLA Modules:
  0.0 144.2 jit_solution(10742335879080661850)
XLA Ops:
  0.0 1.1 fusion.23
  1.1 0.9 fusion.22
  2.0 0.9 fusion.21
  2.9 0.9 fusion.20
  3.8 0.9 fusion.19
  4.8 0.9 fusion.18
  5.7 0.9 fusion.17
  6.6 0.9 fusion.16
  7.5 0.0 copy-done.4
  7.7 0.0 copy-start.3
  7.7 1.3 copy-done.3
  9.0 6.5 %all-to-all-start = ((f32[16,2,1,64,256]{4,3,2,1,0:T(8,128)}), f32[16,2,1,64,256]{4,3,2,1,0:T(8,128)S(1)}, u32[]{:S(2)}, u32[]{:S(2)}) async-start(f32[16,2,1,64,256]{4,3,2,1,0:T(8,128)} %bitcast.149), calls=%async_computation | async-start | bytes 4194304 | tf_op jit(solution)/shard_map/all_to_all | solution.py:49
  15.6 0.1 sine_negate_fusion.4
  15.6 47.3 %all-to-all-done = f32[16,2,1,64,256]{4,3,2,1,0:T(8,128)S(1)} async-done(((f32[16,2,1,64,256]{4,3,2,1,0:T(8,128)}), f32[16,2,1,64,256]{4,3,2,1,0:T(8,128)S(1)}, u32[]{:S(2)}, u32[]{:S(2)}) %all-to-all-start) | async-done | bytes 2097184 | tf_op jit(solution)/shard_map/all_to_all | solution.py:49
  63.0 1.2 fusion.95
  64.1 0.6 copy.130
  64.7 1.3 copy.131
  66.0 1.2 fusion.27
  67.3 2.2 %fusion.31 = f32[128,64,32]{0,1,2:T(8,128)} fusion(f32[64,128,32]{1,0,2:T(8,128)S(1)} %copy.131), kind=kOutput, calls=%fused_computation.59 | convolution fusion | flops 402882560 | bytes 2097152 | tf_op jit(solution)/shard_map/rab,ak->rkb/dot_general | solution.py:18
  69.5 0.0 copy-done.1
  69.5 1.9 %copy.132 = f32[1,1,64,16,256]{2,4,3,1,0:T(8,128)} copy(f32[1,1,64,16,256]{4,2,1,0,3:T(8,128)S(1)} %copy-done.1) | data formatting | bytes 2097152 | tf_op jit(solution)/shard_map/slice | solution.py:20
  71.4 2.7 %copy.133 = f32[64,128,32]{1,0,2:T(8,128)S(1)} copy(f32[64,128,32]{0,2,1:T(8,128)} %bitcast.145) | data formatting | bytes 2097152 | tf_op jit(solution)/shard_map/squeeze | solution.py:20
  74.1 0.0 copy-start
  74.1 1.3 convolution_add_fusion.1
  75.4 0.0 copy-done
  75.4 1.4 add_bitcast_fusion
  76.8 1.6 %fusion.6 = f32[32,64,128]{2,0,1:T(8,128)S(1)} fusion(f32[64,128,32]{1,0,2:T(8,128)S(1)} %get-tuple-element.6), kind=kOutput, calls=%fused_computation.15 | convolution fusion | flops 100677632 | bytes 2097152 | tf_op jit(solution)/shard_map/rkb,bm->rmk/dot_general | solution.py:18
  78.4 1.6 %fusion.4 = f32[32,64,128]{2,0,1:T(8,128)S(1)} fusion(f32[64,128,32]{1,0,2:T(8,128)S(1)} %get-tuple-element.6), kind=kOutput, calls=%fused_computation.13 | convolution fusion | flops 100678656 | bytes 2097152 | tf_op jit(solution)/shard_map/rkb,bm->rmk/dot_general | solution.py:21
  80.0 1.8 %fusion.1 = f32[64,32,128]{2,1,0:T(8,128)S(1)} fusion(f32[32,64,128]{2,0,1:T(8,128)S(1)} %fusion.6, f32[64,128,32]{1,0,2:T(8,128)S(1)} %get-tuple-element.5), kind=kOutput, calls=%fused_computation.5 | convolution fusion | flops 100940800 | bytes 3145728 | tf_op jit(solution)/shard_map/rkb,bm->rmk/dot_general | solution.py:20
  81.8 1.3 stack.77
  83.0 2.8 %copy.140 = f32[1,64,16,256]{3,1,0,2:T(8,128)} copy(f32[1,64,16,256]{3,2,1,0:T(8,128)} %stack.77) | data formatting | bytes 2097152 | tf_op jit(solution)/shard_map/stack | solution.py:24
  85.8 1.6 %fusion = f32[64,32,128]{2,1,0:T(8,128)S(1)} fusion(f32[32,64,128]{2,0,1:T(8,128)S(1)} %fusion.4, f32[64,128,32]{1,0,2:T(8,128)S(1)} %get-tuple-element.5), kind=kOutput, calls=%fused_computation.3 | convolution fusion | flops 100939776 | bytes 3145728 | tf_op jit(solution)/shard_map/rkb,bm->rmk/dot_general | solution.py:23
  87.4 0.0 copy-start.2
  87.5 0.3 stack.78
  87.8 0.6 copy.141
  88.4 0.3 copy-done.2
  88.7 1.5 %pad_maximum_fusion = f32[2,64,16,256]{3,1,0,2:T(8,128)} fusion(f32[1,64,16,256]{3,1,0,2:T(8,128)S(1)} %copy.141, f32[1,64,16,256]{3,1,0,2:T(8,128)S(1)} %copy-done.2), kind=kLoop, calls=%fused_computation | loop fusion | flops 524288 | bytes 4194304 | tf_op jit(solution)/shard_map/stack | solution.py:24
  90.2 4.9 %all-to-all-start.1 = ((f32[2,64,16,256]{3,1,0,2:T(8,128)}), f32[2,64,16,256]{3,1,0,2:T(8,128)S(1)}, u32[]{:S(2)}, u32[]{:S(2)}) async-start(f32[2,64,16,256]{3,1,0,2:T(8,128)} %pad_maximum_fusion), calls=%async_computation.1 | async-start | bytes 4194304 | tf_op jit(solution)/shard_map/all_to_all | solution.py:68
  95.1 0.0 copy-done.6
  95.1 0.0 copy-done.7
  95.1 0.1 select_reduce_fusion
  95.2 0.0 copy-done.5
  95.2 0.1 copy.143
  95.3 0.3 mul.231
  95.6 0.1 copy.169
  95.7 46.8 %all-to-all-done.1 = f32[2,64,16,256]{3,1,0,2:T(8,128)S(1)} async-done(((f32[2,64,16,256]{3,1,0,2:T(8,128)}), f32[2,64,16,256]{3,1,0,2:T(8,128)S(1)}, u32[]{:S(2)}, u32[]{:S(2)}) %all-to-all-start.1) | async-done | bytes 2097184 | tf_op jit(solution)/shard_map/all_to_all | solution.py:68
  142.5 0.2 copy.142
  142.7 1.5 %bitcast_multiply_fusion = f32[2,1024,256]{2,1,0:T(8,128)} fusion(f32[2,64,16,256]{3,1,2,0:T(8,128)S(1)} %copy.142, f32[1024,256]{1,0:T(8,128)S(1)} %bitcast.147), kind=kLoop, calls=%fused_computation.1 | loop fusion | flops 524288 | bytes 5242880 | tf_op jit(solution)/shard_map/mul | solution.py:78
  (14 shorter events, 0.1 us)
Async XLA Ops:
  0.0 7.5 %copy-start.4 = (f32[2,1024,256]{2,1,0:T(8,128)S(1)}, f32[2,1024,256]{2,1,0:T(8,128)}, u32[]{:S(2)}) copy-start(f32[2,1024,256]{2,1,0:T(8,128)} %param.4) | copy-start | bytes 6291460
  7.7 1.3 copy-start.3
  9.0 53.9 %all-to-all-start = ((f32[16,2,1,64,256]{4,3,2,1,0:T(8,128)}), f32[16,2,1,64,256]{4,3,2,1,0:T(8,128)S(1)}, u32[]{:S(2)}, u32[]{:S(2)}) async-start(f32[16,2,1,64,256]{4,3,2,1,0:T(8,128)} %bitcast.149), calls=%async_computation | async-start | bytes 4194304 | tf_op jit(solution)/shard_map/all_to_all | solution.py:49
  66.0 3.5 %copy-start.1 = (f32[1,1,64,16,256]{4,2,1,0,3:T(8,128)S(1)}, f32[1,1,64,16,256]{4,2,1,0,3:T(8,128)}, u32[]{:S(2)}) copy-start(f32[1,1,64,16,256]{4,2,1,0,3:T(8,128)} %get-tuple-element.7) | copy-start | bytes 3145732
  74.1 1.3 copy-start
  87.4 1.2 copy-start.2
  90.1 4.9 %copy-start.6 = (s32[8,2]{0,1:T(2,128)S(1)}, s32[8,2]{0,1:T(2,128)}, u32[]{:S(2)}) copy-start(s32[8,2]{0,1:T(2,128)} %param.6) | copy-start | bytes 196
  90.1 4.9 %copy-start.7 = (f32[4]{0:T(128)S(1)}, f32[4]{0:T(128)}, u32[]{:S(2)}) copy-start(f32[4]{0:T(128)} %param.7) | copy-start | bytes 52
  90.1 5.0 %copy-start.5 = (s32[8,2]{0,1:T(2,128)S(1)}, s32[8,2]{0,1:T(2,128)}, u32[]{:S(2)}) copy-start(s32[8,2]{0,1:T(2,128)} %param.5) | copy-start | bytes 196
  90.2 52.3 %all-to-all-start.1 = ((f32[2,64,16,256]{3,1,0,2:T(8,128)}), f32[2,64,16,256]{3,1,0,2:T(8,128)S(1)}, u32[]{:S(2)}, u32[]{:S(2)}) async-start(f32[2,64,16,256]{3,1,0,2:T(8,128)} %pad_maximum_fusion), calls=%async_computation.1 | async-start | bytes 4194304 | tf_op jit(solution)/shard_map/all_to_all | solution.py:68
